TPU v7x, 32 devices: a whole 2x2x4 slice. The times are simulated.
32 devices in a mesh: dp: 8 (over y, x, core), tensor: 4 (over z).
Axes of the slice: x: 2, y: 2, z: 4, core: 2. Of those that a mesh axis runs over, the one named last changes fastest.
Arguments:
- tokens: bfloat16 [16384, 1536], P('dp'), may hold values from -6 to 6
- lengths: int32 [8], P('dp'), may hold values from 1024 to 2048, as said below
- cotangent: bfloat16 [16384, 1536], P('dp'), may hold values from -6 to 6
- norm_gain: float32 [1536], replicated, may hold values from 0.1 to 1.9
- query_w: bfloat16 [1536, 1536], P(None, 'tensor'), may hold values from -0.15625 to 0.15625
- key_weight: bfloat16 [1536, 512], P(None, 'tensor'), may hold values from -0.15625 to 0.15625
- value_weight: bfloat16 [1536, 512], P(None, 'tensor'), may hold values from -0.15625 to 0.15625
- out_w: bfloat16 [1536, 1536], P('tensor'), may hold values from -0.625 to 0.625
- query_gain: float32 [64], replicated, may hold values from 0.1 to 1.9
- key_gain: float32 [64], replicated, may hold values from 0.1 to 1.9
- mlp_gain: float32 [1536], replicated, may hold values from 0.1 to 1.9
- gate_w: bfloat16 [1536, 6912], P(None, 'tensor'), may hold values from -0.15625 to 0.15625
- up_w: bfloat16 [1536, 6912], P(None, 'tensor'), may hold values from -0.15625 to 0.15625
- down_w: bfloat16 [6912, 1536], P('tensor'), may hold values from -0.078125 to 0.078125
Outputs:
- block_out: bfloat16 [16384, 1536], P('dp')
- input_grad: float32 [16384, 1536], P('dp')
- norm_gain_grad: float32 [1536], replicated
- query_w_grad: float32 [1536, 1536], P(None, 'tensor')
- key_w_grad: float32 [1536, 512], P(None, 'tensor')
- value_weight_gradient: float32 [1536, 512], P(None, 'tensor')
- out_w_grad: float32 [1536, 1536], P('tensor')
- query_gain_grad: float32 [64], replicated
- key_gain_grad: float32 [64], replicated
- mlp_gain_grad: float32 [1536], replicated
- gate_w_grad: float32 [1536, 6912], P(None, 'tensor')
- up_w_grad: float32 [1536, 6912], P(None, 'tensor')
- down_w_grad: float32 [6912, 1536], P('tensor')
Inputs may be any that keep to these rules, and one draw needn't show every extreme that they name: `lengths`: each sequence's live slots are its first ones; some sequence fills all 2048 slots.
All inputs are finite; a program needn't handle non-finite values.
Results may differ from a plain program's by a relative error of at most 0.024.
Values may be sent and summed in bfloat16 or wider, within the bound.
A program may use at most 384 MiB of HBM per device.

v0:
```python
import math
import jax
import jax.numpy as jnp
from jax import lax
from jax.sharding import PartitionSpec as P

HEAD_SIZE = 64
BLK = 512
EPSILON = 1e-05
ROPE_BASE = 1000000.0


def rms_scale(inputs, gain_vec):
    return (
        inputs * lax.rsqrt(jnp.mean(inputs * inputs, axis=-1, keepdims=True) + EPSILON) * gain_vec
    )


def rotary(inputs, head_count):
    row_count = inputs.shape[0]
    half_dim = HEAD_SIZE // 2
    positions = jnp.arange(row_count).astype(jnp.float32)[:, None]
    inv_freq = jnp.exp(
        jnp.arange(half_dim).astype(jnp.float32) * (-2.0 * math.log(ROPE_BASE) / HEAD_SIZE)
    )
    angles = positions * inv_freq[None, :]
    cosine = jnp.cos(angles)[:, None, :]
    sine_tab = jnp.sin(angles)[:, None, :]
    split_heads = inputs.reshape(row_count, head_count, HEAD_SIZE)
    lower_half = split_heads[..., :half_dim]
    upper_half = split_heads[..., half_dim:]
    turned = jnp.concatenate(
        [lower_half * cosine - upper_half * sine_tab, upper_half * cosine + lower_half * sine_tab],
        axis=-1,
    )
    return turned.reshape(row_count, head_count * HEAD_SIZE)


def head_norm(inputs, gain_vec, head_count):
    row_count = inputs.shape[0]
    return rms_scale(inputs.reshape(row_count, head_count, HEAD_SIZE), gain_vec).reshape(
        row_count, head_count * HEAD_SIZE
    )


def prepare(queries, keys_val, q_gain, k_gain):
    q_count = queries.shape[1] // HEAD_SIZE
    kv_count = keys_val.shape[1] // HEAD_SIZE
    return (
        rotary(head_norm(queries, q_gain, q_count), q_count),
        rotary(head_norm(keys_val, k_gain, kv_count), kv_count),
    )


def swiglu(gate_val, up_val):
    return gate_val * jax.nn.sigmoid(gate_val) * up_val


def left_dot(left, right):
    return lax.dot_general(
        left, right, (((0,), (0,)), ((), ())), preferred_element_type=jnp.float32
    )


def right_dot(left, right):
    return lax.dot_general(
        left, right, (((1,), (1,)), ((), ())), preferred_element_type=jnp.float32
    )


def masked_scores(q_block, k_block, first_row, length):
    raw_scores = jnp.einsum("kgqd,kjd->kgqj", q_block, k_block, preferred_element_type=jnp.float32)
    scaled = raw_scores * float(HEAD_SIZE) ** (-0.5)
    query_pos = first_row + jnp.arange(q_block.shape[2], dtype=jnp.int32)
    key_pos = jnp.arange(k_block.shape[1], dtype=jnp.int32)
    allowed = (key_pos[None, :] <= query_pos[:, None]) & (key_pos[None, :] < length)
    return jnp.where(allowed, scaled, -jnp.inf)


def on_device(
    tokens,
    lengths,
    cotangent,
    norm_gain,
    query_w,
    key_weight,
    value_weight,
    out_w,
    query_gain,
    key_gain,
    mlp_gain,
    gate_w,
    up_w,
    down_w,
):
    row_count = tokens.shape[0]
    length = lengths[0]
    live_rows = (jnp.arange(row_count, dtype=jnp.int32) < length).astype(jnp.float32)
    inputs = tokens.astype(jnp.float32)
    normed, norm_pull = jax.vjp(rms_scale, inputs, norm_gain)
    normed_b = normed.astype(jnp.bfloat16)
    queries = jnp.dot(normed_b, query_w, preferred_element_type=jnp.float32)
    keys_val = jnp.dot(normed_b, key_weight, preferred_element_type=jnp.float32)
    values_b = jnp.dot(normed_b, value_weight, preferred_element_type=jnp.float32).astype(
        jnp.bfloat16
    )
    (query_r, keys_r), prep_pull = jax.vjp(prepare, queries, keys_val, query_gain, key_gain)
    kv_count = key_weight.shape[1] // HEAD_SIZE
    group_size = query_w.shape[1] // key_weight.shape[1]
    q_heads = (
        query_r.astype(jnp.bfloat16)
        .reshape(row_count, kv_count, group_size, HEAD_SIZE)
        .transpose(1, 2, 0, 3)
    )
    k_heads = keys_r.astype(jnp.bfloat16).reshape(row_count, kv_count, HEAD_SIZE).transpose(1, 0, 2)
    v_heads = values_b.reshape(row_count, kv_count, HEAD_SIZE).transpose(1, 0, 2)
    block_outs = []
    log_sums = []
    for first_row in range(0, row_count, BLK):
        last_row = first_row + BLK
        scores = masked_scores(
            q_heads[:, :, first_row:last_row], k_heads[:, :last_row], first_row, length
        )
        row_max = jnp.max(scores, axis=-1, keepdims=True)
        weight = jnp.exp(scores - row_max)
        row_sum = jnp.sum(weight, axis=-1, keepdims=True)
        attn_prob = (weight / row_sum).astype(jnp.bfloat16)
        block_outs.append(
            jnp.einsum(
                "kgqj,kjd->kgqd",
                attn_prob,
                v_heads[:, :last_row],
                preferred_element_type=jnp.float32,
            )
        )
        log_sums.append(row_max + jnp.log(row_sum))
    mixed_b = (
        jnp.concatenate(block_outs, axis=2)
        .transpose(2, 0, 1, 3)
        .reshape(row_count, kv_count * group_size * HEAD_SIZE)
        .astype(jnp.bfloat16)
    )
    attn_out = lax.psum(
        jnp.dot(mixed_b, out_w, preferred_element_type=jnp.float32).astype(jnp.bfloat16), "tensor"
    ).astype(jnp.float32)
    residual = inputs + attn_out
    normed2, norm2_pull = jax.vjp(rms_scale, residual, mlp_gain)
    normed2_b = normed2.astype(jnp.bfloat16)
    gate_val = jnp.dot(normed2_b, gate_w, preferred_element_type=jnp.float32)
    up_val = jnp.dot(normed2_b, up_w, preferred_element_type=jnp.float32)
    hidden, glu_pull = jax.vjp(swiglu, gate_val, up_val)
    hidden_b = hidden.astype(jnp.bfloat16)
    mlp_out = lax.psum(
        jnp.dot(hidden_b, down_w, preferred_element_type=jnp.float32).astype(jnp.bfloat16), "tensor"
    ).astype(jnp.float32)
    block_out = (residual + mlp_out).astype(jnp.bfloat16)
    d_out = cotangent.astype(jnp.float32) * live_rows[:, None]
    d_out_b = d_out.astype(jnp.bfloat16)
    d_down = left_dot(hidden_b, d_out_b)
    d_hidden = right_dot(d_out_b, down_w)
    d_gate, d_up = glu_pull(d_hidden)
    d_gate_b = d_gate.astype(jnp.bfloat16)
    d_up_b = d_up.astype(jnp.bfloat16)
    d_gate_w = left_dot(normed2_b, d_gate_b)
    d_up_w = left_dot(normed2_b, d_up_b)
    d_normed2 = lax.psum(
        (right_dot(d_gate_b, gate_w) + right_dot(d_up_b, up_w)).astype(jnp.bfloat16), "tensor"
    ).astype(jnp.float32)
    d_resid_norm, d_mlp_gain = norm2_pull(d_normed2)
    d_resid = d_out + d_resid_norm
    d_resid_b = d_resid.astype(jnp.bfloat16)
    output_weight_cotangent = left_dot(mixed_b, d_resid_b)
    d_mixed = right_dot(d_resid_b, out_w).astype(jnp.bfloat16)
    d_heads = d_mixed.reshape(row_count, kv_count, group_size, HEAD_SIZE).transpose(1, 2, 0, 3)
    d_keys = jnp.zeros((kv_count, row_count, HEAD_SIZE), jnp.float32)
    d_values = jnp.zeros((kv_count, row_count, HEAD_SIZE), jnp.float32)
    d_queries = []
    for block_idx in range(row_count // BLK):
        first_row = block_idx * BLK
        last_row = first_row + BLK
        q_block = q_heads[:, :, first_row:last_row]
        scores = masked_scores(q_block, k_heads[:, :last_row], first_row, length)
        attn_prob = jnp.exp(scores - log_sums[block_idx])
        d_block = d_heads[:, :, first_row:last_row]
        d_values = d_values.at[:, :last_row].add(
            jnp.einsum(
                "kgqj,kgqd->kjd",
                attn_prob.astype(jnp.bfloat16),
                d_block,
                preferred_element_type=jnp.float32,
            )
        )
        d_prob = jnp.einsum(
            "kgqd,kjd->kgqj", d_block, v_heads[:, :last_row], preferred_element_type=jnp.float32
        )
        spread = jnp.sum(attn_prob * d_prob, axis=-1, keepdims=True)
        d_scores = (attn_prob * (d_prob - spread) * float(HEAD_SIZE) ** (-0.5)).astype(jnp.bfloat16)
        d_queries.append(
            jnp.einsum(
                "kgqj,kjd->kgqd",
                d_scores,
                k_heads[:, :last_row],
                preferred_element_type=jnp.float32,
            )
        )
        d_keys = d_keys.at[:, :last_row].add(
            jnp.einsum("kgqj,kgqd->kjd", d_scores, q_block, preferred_element_type=jnp.float32)
        )
    d_query_r = (
        jnp.concatenate(d_queries, axis=2)
        .transpose(2, 0, 1, 3)
        .reshape(row_count, kv_count * group_size * HEAD_SIZE)
    )
    d_keys_r = d_keys.transpose(1, 0, 2).reshape(row_count, kv_count * HEAD_SIZE)
    d_values_b = (
        d_values.transpose(1, 0, 2).reshape(row_count, kv_count * HEAD_SIZE).astype(jnp.bfloat16)
    )
    d_query_f, d_keys_f, d_qgain, d_kgain = prep_pull((d_query_r, d_keys_r))
    d_query_b = d_query_f.astype(jnp.bfloat16)
    d_keys_b = d_keys_f.astype(jnp.bfloat16)
    d_query_w = left_dot(normed_b, d_query_b)
    d_key_w = left_dot(normed_b, d_keys_b)
    d_value_w = left_dot(normed_b, d_values_b)
    d_normed = lax.psum(
        (
            right_dot(d_query_b, query_w)
            + right_dot(d_keys_b, key_weight)
            + right_dot(d_values_b, value_weight)
        ).astype(jnp.bfloat16),
        "tensor",
    ).astype(jnp.float32)
    d_input_norm, norm_gain_cotangent = norm_pull(d_normed)
    d_inputs = d_resid + d_input_norm
    head_totals = lax.psum((d_qgain, d_kgain), ("dp", "tensor"))
    all_totals = (
        lax.psum(norm_gain_cotangent.astype(jnp.bfloat16), "dp").astype(jnp.float32),
        lax.psum(d_query_w.astype(jnp.bfloat16), "dp").astype(jnp.float32),
        lax.psum(d_key_w.astype(jnp.bfloat16), "dp").astype(jnp.float32),
        lax.psum(d_value_w.astype(jnp.bfloat16), "dp").astype(jnp.float32),
        lax.psum(output_weight_cotangent.astype(jnp.bfloat16), "dp").astype(jnp.float32),
        lax.psum(d_gate_w.astype(jnp.bfloat16), "dp").astype(jnp.float32),
        lax.psum(d_up_w.astype(jnp.bfloat16), "dp").astype(jnp.float32),
        lax.psum(d_down.astype(jnp.bfloat16), "dp").astype(jnp.float32),
        lax.psum(d_mlp_gain.astype(jnp.bfloat16), "dp").astype(jnp.float32),
    )
    g_norm, g_query, g_key, g_value, g_out, g_gate, g_up, g_down, g_mlp = all_totals
    return (
        block_out,
        d_inputs,
        g_norm,
        g_query,
        g_key,
        g_value,
        g_out,
        head_totals[0],
        head_totals[1],
        g_mlp,
        g_gate,
        g_up,
        g_down,
    )


def solution(mesh):
    return jax.shard_map(
        on_device,
        mesh=mesh,
        in_specs=(
            P("dp", None),
            P("dp"),
            P("dp", None),
            P(),
            P(None, "tensor"),
            P(None, "tensor"),
            P(None, "tensor"),
            P("tensor", None),
            P(),
            P(),
            P(),
            P(None, "tensor"),
            P(None, "tensor"),
            P("tensor", None),
        ),
        out_specs=(
            P("dp", None),
            P("dp", None),
            P(),
            P(None, "tensor"),
            P(None, "tensor"),
            P(None, "tensor"),
            P("tensor", None),
            P(),
            P(),
            P(),
            P(None, "tensor"),
            P(None, "tensor"),
            P("tensor", None),
        ),
        check_vma=False,
    )
```

profile of v0, /device:TPU:0, one launch (start us, length us, event | category | flops | bytes accessed | tf_op | source)
XLA Modules:
  0.0 1743.3 jit_solution(18047508188142419568)
XLA Ops:
  116.9 223.2 %all-reduce.15.cloned.1.call-done = bf16[2048,1536]{1,0:T(8,128)(2,1)} async-done(((bf16[2048,1536]{1,0:T(8,128)(2,1)}), bf16[2048,1536]{1,0:T(8,128)(2,1)}) %all-reduce.15.cloned.1.call-update) | async-done | bytes 6291472 | tf_op jit(solution)/shard_map/psum | solution.py:143
  353.2 16.7 fusion.282
  369.9 13.7 fusion.281
  383.6 28.7 %multiply_convert_fusion.2 = (bf16[2048,1728]{0,1:T(8,128)(2,1)}, bf16[2048,1728]{0,1:T(8,128)(2,1)}, bf16[2048,1728]{0,1:T(8,128)(2,1)}) fusion(f32[2048,1728]{0,1:T(8,128)} %fusion.281, f32[2048,1728]{0,1:T(8,128)} %fusion.282, bf16[1728,1536]{1,0:T(8,128)(2,1)} %param.47, bf16[2048,1536]{1,0:T(8,128)(2,1)} %param.36, f32[2048]{0:T(1024)S(1)} %fusion.239), kind=kOutput, calls=%fused_computation.41 | convolution fusion | flops 10937696256 | bytes 61153280 | tf_op jit(solution)/shard_map/dot_general | solution.py:66
  412.3 16.5 fusion.283
  428.8 17.7 %add_convert_fusion.1 = bf16[2048,1536]{1,0:T(8,128)(2,1)} fusion(f32[2048,1536]{1,0:T(8,128)S(1)} %fusion.283, bf16[2048,1728]{0,1:T(8,128)(2,1)} %get-tuple-element.146, bf16[1536,1728]{0,1:T(8,128)(2,1)} %param.46), kind=kOutput, calls=%fused_computation.63 | convolution fusion | flops 10877927424 | bytes 31260672 | tf_op jit(solution)/shard_map/dot_general | solution.py:66
  446.5 17.0 convolution_convert_fusion
  463.5 16.9 convolution_convert_fusion.1
  480.4 13.3 convolution_convert_fusion.2
  493.8 174.6 %all-reduce.17.cloned.1.call-done = bf16[2048,1536]{1,0:T(8,128)(2,1)} async-done(((bf16[2048,1536]{1,0:T(8,128)(2,1)}), bf16[2048,1536]{1,0:T(8,128)(2,1)}) %all-reduce.17.cloned.1.call-update) | async-done | bytes 6291472 | tf_op jit(solution)/shard_map/psum | solution.py:166
  715.0 12.1 fusion.116
  780.0 33.9 %fusion.84 = f32[2,3,512,64]{2,3,1,0:T(8,128)} fusion(f32[2,3,512,1024]{3,2,1,0:T(8,128)} %fusion.220, f32[2,3,512,1024]{3,2,1,0:T(8,128)} %copy-done.11, f32[2,3,512]{2,1,0:T(4,128)S(1)} %copy-done.79, pred[512,1024]{1,0:T(8,128)(4,1)} %copy-done.22, bf16[2,2048,64]{1,2,0:T(8,128)(2,1)S(1)} %copy-done.47), kind=kOutput, calls=%fused_computation.99 | convolution fusion | flops 437260288 | bytes 52461568 | tf_op jit(solution)/shard_map/kgqj,kjd->kgqd/dot_general | solution.py:199
  813.9 34.6 %fusion.193 = f32[2,2048,64]{1,2,0:T(8,128)} fusion(f32[2,2048,64]{1,2,0:T(8,128)} %scatter-add.20, f32[2,3,512,1024]{3,2,1,0:T(8,128)} %fusion.220, f32[2,3,512,1024]{3,2,1,0:T(8,128)} %copy-done.11, f32[2,3,512]{2,1,0:T(4,128)S(1)} %copy-done.79, pred[512,1024]{1,0:T(8,128)(4,1)} %copy-done.22, bf16[2,3,2048,64]{2,3,1,0:T(8,128)(2,1)S(1)} %bitcast.225), kind=kOutput, calls=%fused_computation.180 | convolution fusion | flops 437391360 | bytes 52854784 | tf_op jit(solution)/shard_map/kgqj,kgqd->kjd/dot_general | solution.py:207
  848.5 29.6 %fusion.63 = f32[2,3,512,64]{2,3,1,0:T(8,128)} fusion(f32[2,3,512,1536]{3,2,1,0:T(8,128)} %fusion.217, f32[2,3,512,1536]{3,2,1,0:T(8,128)} %get-tuple-element.166, f32[2,3,512]{2,1,0:T(4,128)S(1)} %copy-done.77, bf16[2,2048,64]{1,2,0:T(8,128)(2,1)S(1)} %copy-done.47), kind=kOutput, calls=%fused_computation.82 | convolution fusion | flops 637014528 | bytes 76709888 | tf_op jit(solution)/shard_map/kgqj,kjd->kgqd/dot_general | solution.py:199
  878.1 30.0 %fusion.167 = f32[2,2048,64]{1,2,0:T(8,128)} fusion(f32[2,2048,64]{1,2,0:T(8,128)} %fusion.193, f32[2,3,512,1536]{3,2,1,0:T(8,128)} %fusion.217, f32[2,3,512,1536]{3,2,1,0:T(8,128)} %get-tuple-element.166, f32[2,3,512]{2,1,0:T(4,128)S(1)} %copy-done.77, bf16[2,3,2048,64]{2,3,1,0:T(8,128)(2,1)S(1)} %bitcast.226), kind=kOutput, calls=%fused_computation.157 | convolution fusion | flops 637211136 | bytes 77496320 | tf_op jit(solution)/shard_map/kgqj,kgqd->kjd/dot_general | solution.py:207
  908.2 45.0 %fusion.27 = f32[2,3,512,64]{2,3,1,0:T(8,128)} fusion(f32[2,3,512,2048]{3,2,1,0:T(8,128)} %fusion.214, f32[2,3,512,2048]{3,2,1,0:T(8,128)} %get-tuple-element.164, f32[2,3,512]{2,1,0:T(4,128)S(1)} %copy-done.78, pred[512,2048]{1,0:T(8,128)(4,1)} %copy-done.20, bf16[2048,2,32]{0,2,1:T(8,128)(2,1)S(1)} %copy-done.41, bf16[2048,2,32]{0,2,1:T(8,128)(2,1)S(1)} %copy-done.38), kind=kOutput, calls=%fused_computation.47 | convolution fusion | flops 875566080 | bytes 52703232 | tf_op jit(solution)/shard_map/kgqj,kjd->kgqd/dot_general | solution.py:199
  953.2 48.7 %fusion.173 = f32[2048,2,64]{0,2,1:T(8,128)} fusion(f32[2,2048,64]{1,2,0:T(8,128)} %fusion.167, f32[2,3,512,2048]{3,2,1,0:T(8,128)} %fusion.214, f32[2,3,512,2048]{3,2,1,0:T(8,128)} %get-tuple-element.164, f32[2,3,512]{2,1,0:T(4,128)S(1)} %copy-done.78, pred[512,2048]{1,0:T(8,128)(4,1)} %copy-done.20, bf16[2,3,2048,64]{2,3,1,0:T(8,128)(2,1)S(1)} %bitcast.227), kind=kOutput, calls=%fused_computation.159 | convolution fusion | flops 874779648 | bytes 105283584 | tf_op jit(solution)/shard_map/kgqj,kgqd->kjd/dot_general | solution.py:207
  1016.6 17.4 convolution_convert_fusion.3
  1047.0 13.2 add_convert_fusion
  1060.3 40.8 %all-reduce.6 = (f32[64]{0:T(128)}, f32[64]{0:T(128)}) all-reduce(f32[64]{0:T(128)S(1)} %get-tuple-element.129, f32[64]{0:T(128)S(1)} %get-tuple-element.131), channel_id=1, replica_groups=mesh['dp'=8,'tensor'=4] {'dp','tensor'}, use_global_device_ids=true, to_apply=%region_31.32 | all-reduce | flops 128 | bytes 1024 | tf_op jit(solution)/shard_map/psum | solution.py:234
  1101.1 160.8 %all-reduce.19.cloned.1.call-done = (bf16[1536,384]{1,0:T(8,128)(2,1)}, bf16[1536,128]{1,0:T(8,128)(2,1)}, bf16[1536,128]{1,0:T(8,128)(2,1)}, bf16[384,1536]{1,0...) async-done(((bf16[1536,384]{1,0:T(8,128)(2,1)}, bf16[1536,128]{1,0:T(8,128)(2,1)}, bf16[1536,128]{1,0:T(8,128)(2,1)}, ...) | async-done | bytes 19070992 | tf_op jit(solution)/shard_map/psum | solution.py:237
  1288.8 403.2 %all-reduce.21.cloned.1.call-done = (bf16[2048,1536]{1,0:T(8,128)(2,1)}, bf16[2048,1536]{1,0:T(8,128)(2,1)}) async-done(((bf16[2048,1536]{1,0:T(8,128)(2,1)}, bf16[2048,1536]{1,0:T(8,128)(2,1)}), (bf16[2048,1536]{1,0:T(8,128)(2,1)}, bf16[2048,1536]{1,0:T(8,128)(2,1)})) %all-reduce.21.cloned.1.call-update) | async-done | bytes 12582928 | tf_op jit(solution)/shard_map/psum | solution.py:153
  1700.2 13.9 all-reduce.7
  1715.4 20.9 %fusion.34 = (f32[2048,1536]{1,0:T(8,128)}, bf16[2048,1536]{1,0:T(8,128)(2,1)}) fusion(f32[2048,1536]{1,0:T(8,128)} %copy-done.6, bf16[2048,1536]{1,0:T(8,128)(2,1)} %get-tuple-element.145, bf16[2048,1536]{1,0:T(8,128)(2,1)} %param.34, f32[2048]{0:T(1024)S(1)} %multiply_multiply_fusion.4, f32[1536]{0:T(1024)S(1)} %copy-done.59, f32[2048]{0:T(1024)S(1)} %copy-done.56, ...), kind=kLoop, calls=%fused_computation.53 | loop fusion | flops 40894464 | bytes 56645632 | tf_op jit(solution)/shard_map/add | solution.py:233
  (321 shorter events, 284.1 us)
Async XLA Ops:
  7.2 101.7 %copy-start = (bf16[384,1536]{1,0:T(8,128)(2,1)S(1)}, bf16[384,1536]{1,0:T(8,128)(2,1)}, u32[]{:S(2)}) copy-start(bf16[384,1536]{1,0:T(8,128)(2,1)} %param.41) | copy-start | bytes 3538948
  7.2 332.9 %all-reduce.15.cloned.1.call-start = ((), (), s32[]{:S(2)}) async-start(), calls=%async_computation | async-start | bytes 12582912 | tf_op jit(solution)/shard_map/psum | solution.py:143
  19.2 76.7 %copy-start.12 = (bf16[2048,128]{0,1:T(8,128)(2,1)}, bf16[2048,128]{0,1:T(8,128)(2,1)S(1)}, u32[]{:S(2)}) copy-start(bf16[2048,128]{0,1:T(8,128)(2,1)S(1)} %convolution_convert_fusion.6) | copy-start | bytes 1572868
  27.7 45.6 %copy-start.37 = (bf16[2048,2,32]{0,2,1:T(8,128)(2,1)}, bf16[2048,2,32]{0,2,1:T(8,128)(2,1)S(1)}, u32[]{:S(2)}) copy-start(bf16[2048,2,32]{0,2,1:T(8,128)(2,1)S(1)} %get-tuple-element.157) | copy-start | bytes 786436
  28.8 44.5 %copy-start.28 = (bf16[2048,6,64]{0,2,1:T(8,128)(2,1)}, bf16[2048,6,64]{0,2,1:T(8,128)(2,1)S(1)}, u32[]{:S(2)}) copy-start(bf16[2048,6,64]{0,2,1:T(8,128)(2,1)S(1)} %pad_maximum_fusion.1) | copy-start | bytes 4718596
  73.4 22.5 %copy-start.20 = (pred[512,2048]{1,0:T(8,128)(4,1)}, pred[512,2048]{1,0:T(8,128)(4,1)S(1)}, u32[]{:S(2)}) copy-start(pred[512,2048]{1,0:T(8,128)(4,1)S(1)} %fusion.111) | copy-start | bytes 3145732
  114.4 233.2 %copy-start.64 = (f32[1536]{0:T(1024)S(1)}, f32[1536]{0:T(1024)}, u32[]{:S(2)}) copy-start(f32[1536]{0:T(1024)} %param.44) | copy-start | bytes 18436
  114.4 554.0 %all-reduce.17.cloned.1.call-start = ((), (), s32[]{:S(2)}) async-start(), calls=%async_computation.1 | async-start | bytes 12582912 | tf_op jit(solution)/shard_map/psum | solution.py:166
  446.4 815.5 %all-reduce.19.cloned.1.call-start = ((), (), s32[]{:S(2)}) async-start(), calls=%async_computation.2 | async-start | bytes 38141952 | tf_op jit(solution)/shard_map/psum | solution.py:237
  446.5 33.9 %slice-start.9 = ((s8[6291456]{0:T(1024)(128)(4,1)}), s8[4194304]{0:T(1024)(128)(4,1)S(1)}, s32[]{:S(2)}) async-start(s8[6291456]{0:T(1024)(128)(4,1)} %bitcast.204), calls=%async_computation.13 | async-start | bytes 8388608
  446.5 33.9 %slice-start.17 = ((s8[7077888]{0:T(1024)(128)(4,1)}), s8[4194304]{0:T(1024)(128)(4,1)S(1)}, s32[]{:S(2)}) async-start(s8[7077888]{0:T(1024)(128)(4,1)} %bitcast.234), calls=%async_computation.21 | async-start | bytes 8388608
  480.4 188.0 %copy-start.58 = (f32[2048]{0:T(1024)S(1)}, f32[2048]{0:T(1024)}, u32[]{:S(2)}) copy-start(f32[2048]{0:T(1024)} %copy-done.57) | copy-start | bytes 24580
  480.4 188.0 %copy-start.65 = (f32[1536]{0:T(1024)S(1)}, f32[1536]{0:T(1024)}, u32[]{:S(2)}) copy-start(f32[1536]{0:T(1024)} %param.44) | copy-start | bytes 18436
  493.8 185.0 %copy-start.63 = (f32[2048]{0:T(1024)S(1)}, f32[2048]{0:T(1024)}, u32[]{:S(2)}) copy-start(f32[2048]{0:T(1024)} %copy-done.62) | copy-start | bytes 24580
  780.0 33.9 %copy-start.29 = (bf16[2048,6,64]{0,2,1:T(8,128)(2,1)S(1)}, bf16[2048,6,64]{0,2,1:T(8,128)(2,1)}, u32[]{:S(2)}) copy-start(bf16[2048,6,64]{0,2,1:T(8,128)(2,1)} %copy-done.28) | copy-start | bytes 4718596
  878.1 30.0 %copy-start.38 = (bf16[2048,2,32]{0,2,1:T(8,128)(2,1)S(1)}, bf16[2048,2,32]{0,2,1:T(8,128)(2,1)}, u32[]{:S(2)}) copy-start(bf16[2048,2,32]{0,2,1:T(8,128)(2,1)} %copy-done.37) | copy-start | bytes 786436
  878.1 30.0 %copy-start.41 = (bf16[2048,2,32]{0,2,1:T(8,128)(2,1)S(1)}, bf16[2048,2,32]{0,2,1:T(8,128)(2,1)}, u32[]{:S(2)}) copy-start(bf16[2048,2,32]{0,2,1:T(8,128)(2,1)} %copy-done.39) | copy-start | bytes 786436
  953.2 51.1 %copy-start.15 = (f32[2048,32]{0,1:T(8,128)S(1)}, f32[2048,32]{0,1:T(8,128)}, u32[]{:S(2)}) copy-start(f32[2048,32]{0,1:T(8,128)} %copy-done.14) | copy-start | bytes 786436
  953.2 51.1 %copy-start.17 = (f32[2048,32]{0,1:T(8,128)S(1)}, f32[2048,32]{0,1:T(8,128)}, u32[]{:S(2)}) copy-start(f32[2048,32]{0,1:T(8,128)} %copy-done.16) | copy-start | bytes 786436
  1016.5 675.5 %all-reduce.21.cloned.1.call-start = ((), (), s32[]{:S(2)}) async-start(), calls=%async_computation.3 | async-start | bytes 25165824 | tf_op jit(solution)/shard_map/psum | solution.py:153
  1283.2 408.8 %copy-start.56 = (f32[2048]{0:T(1024)S(1)}, f32[2048]{0:T(1024)}, u32[]{:S(2)}) copy-start(f32[2048]{0:T(1024)} %copy-done.55) | copy-start | bytes 24580
  1283.2 408.8 %copy-start.59 = (f32[1536]{0:T(1024)S(1)}, f32[1536]{0:T(1024)}, u32[]{:S(2)}) copy-start(f32[1536]{0:T(1024)} %param.37) | copy-start | bytes 18436
  1288.8 411.4 %copy-start.61 = (f32[2048]{0:T(1024)S(1)}, f32[2048]{0:T(1024)}, u32[]{:S(2)}) copy-start(f32[2048]{0:T(1024)} %copy-done.60) | copy-start | bytes 24580
  1288.8 411.4 %copy-start.80 = (bf16[1536]{0:T(1024)(128)(2,1)S(1)}, bf16[1536]{0:T(1024)(128)(2,1)}, u32[]{:S(2)}) copy-start(bf16[1536]{0:T(1024)(128)(2,1)} %get-tuple-element.125) | copy-start | bytes 9220
  (86 other events, 604.9 us)
Sparse Core Ops, SparseCore 0:
  114.5 225.5 all-reduce.14
  446.6 221.7 all-reduce.16
  1016.6 245.2 all-reduce.18
  1265.0 426.9 all-reduce.20
where the time goes:
time: 1750 us; the launch traced here: 1740 us
  waiting for transfers between devices  962 us (55%)
  matrix products  563 us (32%)
  other arithmetic  137 us (8%)
  blocking collectives  54.8 us (3%)
    psum x1, waiting for transfers between devices, on_device(): lax.psum(jnp.dot(hidden_b, down_w, preferred_element_type=jnp.float32).as...  403 us
    psum x1, waiting for transfers between devices, on_device(): lax.psum(jnp.dot(mixed_b, out_w, preferred_element_type=jnp.float32).asty...  223 us
    psum x1, waiting for transfers between devices, on_device(): lax.psum((right_dot(d_gate_b, gate_w) + right_dot(d_up_b, up_w)).astype(j...  175 us
    psum x1, waiting for transfers between devices, on_device(): lax.psum(d_query_w.astype(jnp.bfloat16), 'dp').astype(jnp.float32)  161 us
    dot_general x4, matrix products, on_device(): jnp.einsum('kgqj,kgqd->kjd', d_scores, q_block, preferred_element_type=jn...  125 us
    dot_general x4, matrix products, on_device(): jnp.einsum('kgqj,kjd->kgqd', d_scores, k_heads[:, :last_row], preferred_e...  121 us
    dot_general x7, matrix products, right_dot(): lax.dot_general(left, right, (((1,), (1,)), ((), ())), preferred_element_...  91.9 us
    dot_general x7, matrix products, left_dot(): lax.dot_general(left, right, (((0,), (0,)), ((), ())), preferred_element_...  60.6 us
  transfers between devices with their start and end apart: 4, of which 4 were waited for; matrix products, arithmetic and copies ran while one was open for 7% of the time, Pallas kernels for 0%

commit v1 on v0

--- a/solution.py
+++ b/solution.py
@@ -8,6 +8,11 @@
 BLK = 512
 EPSILON = 1e-05
 ROPE_BASE = 1000000.0
+
+
+def gather_and_add(x, axis):
+    parts = lax.all_gather(x, axis)
+    return jnp.sum(parts, axis=0)
 
 
 def rms_scale(inputs, gain_vec):
@@ -234,7 +239,7 @@
     head_totals = lax.psum((d_qgain, d_kgain), ("dp", "tensor"))
     all_totals = (
         lax.psum(norm_gain_cotangent.astype(jnp.bfloat16), "dp").astype(jnp.float32),
-        lax.psum(d_query_w.astype(jnp.bfloat16), "dp").astype(jnp.float32),
+        gather_and_add(d_query_w.astype(jnp.bfloat16), "dp").astype(jnp.float32),
         lax.psum(d_key_w.astype(jnp.bfloat16), "dp").astype(jnp.float32),
         lax.psum(d_value_w.astype(jnp.bfloat16), "dp").astype(jnp.float32),
         lax.psum(output_weight_cotangent.astype(jnp.bfloat16), "dp").astype(jnp.float32),

time: 1750 us -> 1630 us (0.931)
  waiting for transfers between devices: 962 us -> 832 us
    psum x1, waiting for transfers between devices: 161 us -> 12.7 us  [on_device(): lax.psum(d_key_w.astype(jnp.bfloat16), 'dp').astype(jnp.float32)]
  transfers between devices with their start and end apart: 4 -> 5, of which waited for: 4 -> 5; matrix products, arithmetic and copies ran while one was open for 7% -> 17% of each run, Pallas kernels for 0% -> 0%
where the time goes in v1:
time: 1630 us; the launch traced here: 1620 us
  waiting for transfers between devices  832 us (51%)
  matrix products  564 us (35%)
  other arithmetic  143 us (9%)
  blocking collectives  55 us (3%)
  between operations  16.7 us (1%)
    psum x1, waiting for transfers between devices, on_device(): lax.psum(jnp.dot(hidden_b, down_w, preferred_element_type=jnp.float32).as...  406 us
    psum x1, waiting for transfers between devices, on_device(): lax.psum(jnp.dot(mixed_b, out_w, preferred_element_type=jnp.float32).asty...  223 us
    psum x1, waiting for transfers between devices, on_device(): lax.psum((right_dot(d_gate_b, gate_w) + right_dot(d_up_b, up_w)).astype(j...  175 us
    dot_general x4, matrix products, on_device(): jnp.einsum('kgqj,kjd->kgqd', d_scores, k_heads[:, :last_row], preferred_e...  123 us
    dot_general x4, matrix products, on_device(): jnp.einsum('kgqj,kgqd->kjd', d_scores, q_block, preferred_element_type=jn...  118 us
    dot_general x7, matrix products, right_dot(): lax.dot_general(left, right, (((1,), (1,)), ((), ())), preferred_element_...  91.3 us
    dot_general x7, matrix products, left_dot(): lax.dot_general(left, right, (((0,), (0,)), ((), ())), preferred_element_...  66.9 us
    psum x1, blocking collectives, on_device(): head_totals = lax.psum((d_qgain, d_kgain), ('dp', 'tensor'))  40.1 us
  transfers between devices with their start and end apart: 5, of which 5 were waited for; matrix products, arithmetic and copies ran while one was open for 17% of the time, Pallas kernels for 0%

profile of v1, /device:TPU:0, one launch (start us, length us, event | category | flops | bytes accessed | tf_op | source)
XLA Modules:
  0.0 1619.2 jit_solution(13675303825422726870)
XLA Ops:
  117.1 223.2 %all-reduce.15.cloned.1.call-done = bf16[2048,1536]{1,0:T(8,128)(2,1)} async-done(((bf16[2048,1536]{1,0:T(8,128)(2,1)}), bf16[2048,1536]{1,0:T(8,128)(2,1)}) %all-reduce.15.cloned.1.call-update) | async-done | bytes 6291472 | tf_op jit(solution)/shard_map/psum | solution.py:148
  353.3 16.7 %fusion.282 = f32[2048,1728]{0,1:T(8,128)} fusion(bf16[2048,1536]{1,0:T(8,128)(2,1)S(1)} %multiply_convert_fusion.5, bf16[1536,1728]{0,1:T(8,128)(2,1)} %param.46), kind=kOutput, calls=%fused_computation.291 | convolution fusion | flops 10871635968 | bytes 25755648 | tf_op jit(solution)/shard_map/dot_general | solution.py:155
  370.1 13.7 fusion.281
  383.8 28.7 %multiply_convert_fusion.2 = (bf16[2048,1728]{0,1:T(8,128)(2,1)}, bf16[2048,1728]{0,1:T(8,128)(2,1)}, bf16[2048,1728]{0,1:T(8,128)(2,1)}) fusion(f32[2048,1728]{0,1:T(8,128)} %fusion.281, f32[2048,1728]{0,1:T(8,128)} %fusion.282, bf16[1728,1536]{1,0:T(8,128)(2,1)} %param.47, bf16[2048,1536]{1,0:T(8,128)(2,1)} %param.36, f32[2048]{0:T(1024)S(1)} %fusion.239), kind=kOutput, calls=%fused_computation.41 | convolution fusion | flops 10937696256 | bytes 61153280 | tf_op jit(solution)/shard_map/dot_general | solution.py:71
  412.5 16.5 %fusion.283 = f32[2048,1536]{1,0:T(8,128)S(1)} fusion(bf16[2048,1728]{0,1:T(8,128)(2,1)} %get-tuple-element.146, bf16[1536,1728]{0,1:T(8,128)(2,1)} %param.45), kind=kOutput, calls=%fused_computation.292 | convolution fusion | flops 10871635968 | bytes 24969216 | tf_op jit(solution)/shard_map/dot_general | solution.py:71
  428.9 17.7 %add_convert_fusion.1 = bf16[2048,1536]{1,0:T(8,128)(2,1)} fusion(f32[2048,1536]{1,0:T(8,128)S(1)} %fusion.283, bf16[2048,1728]{0,1:T(8,128)(2,1)} %get-tuple-element.145, bf16[1536,1728]{0,1:T(8,128)(2,1)} %param.46), kind=kOutput, calls=%fused_computation.63 | convolution fusion | flops 10877927424 | bytes 31260672 | tf_op jit(solution)/shard_map/dot_general | solution.py:71
  446.7 17.0 %convolution_convert_fusion = bf16[1536,1728]{0,1:T(8,128)(2,1)} fusion(bf16[2048,1728]{0,1:T(8,128)(2,1)} %get-tuple-element.145, bf16[2048,1536]{1,0:T(8,128)(2,1)} %copy-done.18), kind=kOutput, calls=%fused_computation.92 | convolution fusion | flops 10874290176 | bytes 18677760 | tf_op jit(solution)/shard_map/dot_general | solution.py:65
  463.7 16.8 %convolution_convert_fusion.1 = bf16[1536,1728]{0,1:T(8,128)(2,1)} fusion(bf16[2048,1728]{0,1:T(8,128)(2,1)} %get-tuple-element.146, bf16[2048,1536]{1,0:T(8,128)(2,1)} %copy-done.18), kind=kOutput, calls=%fused_computation.93 | convolution fusion | flops 10874290176 | bytes 18677760 | tf_op jit(solution)/shard_map/dot_general | solution.py:65
  480.6 13.3 convolution_convert_fusion.2
  493.9 174.6 %all-reduce.17.cloned.1.call-done = bf16[2048,1536]{1,0:T(8,128)(2,1)} async-done(((bf16[2048,1536]{1,0:T(8,128)(2,1)}), bf16[2048,1536]{1,0:T(8,128)(2,1)}) %all-reduce.17.cloned.1.call-update) | async-done | bytes 6291472 | tf_op jit(solution)/shard_map/psum | solution.py:171
  768.1 27.3 %fusion.193 = f32[2,2048,64]{1,2,0:T(8,128)} fusion(f32[2,2048,64]{1,2,0:T(8,128)} %scatter-add.20, f32[2,3,512,1024]{3,2,1,0:T(8,128)} %fusion.220, f32[2,3,512,1024]{3,2,1,0:T(8,128)} %copy-done.11, f32[2,3,512]{2,1,0:T(4,128)} %log_add_fusion.2, pred[512,1024]{1,0:T(8,128)(4,1)S(1)} %copy-done.23, bf16[2,3,2048,64]{2,3,1,0:T(8,128)(2,1)S(1)} %bitcast.226), kind=kOutput, calls=%fused_computation.180 | convolution fusion | flops 437391360 | bytes 52854784 | tf_op jit(solution)/shard_map/kgqj,kgqd->kjd/dot_general | solution.py:212
  795.4 30.1 %fusion.167 = f32[2,2048,64]{1,2,0:T(8,128)} fusion(f32[2,2048,64]{1,2,0:T(8,128)} %fusion.193, f32[2,3,512,1536]{3,2,1,0:T(8,128)} %fusion.217, f32[2,3,512,1536]{3,2,1,0:T(8,128)} %get-tuple-element.165, f32[2,3,512]{2,1,0:T(4,128)S(1)} %copy-done.76, bf16[2,3,2048,64]{2,3,1,0:T(8,128)(2,1)S(1)} %bitcast.227), kind=kOutput, calls=%fused_computation.157 | convolution fusion | flops 637211136 | bytes 77496320 | tf_op jit(solution)/shard_map/kgqj,kgqd->kjd/dot_general | solution.py:212
  825.5 48.8 %fusion.173 = f32[2048,2,64]{0,2,1:T(8,128)} fusion(f32[2,2048,64]{1,2,0:T(8,128)} %fusion.167, f32[2,3,512,2048]{3,2,1,0:T(8,128)} %fusion.214, f32[2,3,512,2048]{3,2,1,0:T(8,128)} %get-tuple-element.163, f32[2,3,512]{2,1,0:T(4,128)S(1)} %copy-done.78, pred[512,2048]{1,0:T(8,128)(4,1)} %copy-done.20, bf16[2,3,2048,64]{2,3,1,0:T(8,128)(2,1)} %bitcast.224), kind=kOutput, calls=%fused_computation.159 | convolution fusion | flops 874779648 | bytes 105283584 | tf_op jit(solution)/shard_map/kgqj,kgqd->kjd/dot_general | solution.py:212
  881.9 17.4 %convolution_convert_fusion.3 = bf16[2048,1536]{1,0:T(8,128)(2,1)} fusion(bf16[2048,1728]{0,1:T(8,128)(2,1)} %get-tuple-element.147, bf16[1728,1536]{1,0:T(8,128)(2,1)} %param.47), kind=kOutput, calls=%fused_computation.95 | convolution fusion | flops 10874781696 | bytes 18677760 | tf_op jit(solution)/shard_map/dot_general | solution.py:159
  911.8 34.4 %fusion.84 = f32[2,3,512,64]{2,3,1,0:T(8,128)} fusion(f32[2,3,512,1024]{3,2,1,0:T(8,128)} %fusion.220, f32[2,3,512,1024]{3,2,1,0:T(8,128)} %copy-done.11, f32[2,3,512]{2,1,0:T(4,128)} %log_add_fusion.2, pred[512,1024]{1,0:T(8,128)(4,1)} %copy-done.22, bf16[2,2048,64]{1,2,0:T(8,128)(2,1)S(1)} %copy-done.46), kind=kOutput, calls=%fused_computation.99 | convolution fusion | flops 437260288 | bytes 52461568 | tf_op jit(solution)/shard_map/kgqj,kjd->kgqd/dot_general | solution.py:204
  946.3 30.9 %fusion.63 = f32[2,3,512,64]{2,3,1,0:T(8,128)} fusion(f32[2,3,512,1536]{3,2,1,0:T(8,128)} %fusion.217, f32[2,3,512,1536]{3,2,1,0:T(8,128)} %get-tuple-element.165, f32[2,3,512]{2,1,0:T(4,128)S(1)} %copy-done.76, bf16[2,2048,64]{1,2,0:T(8,128)(2,1)S(1)} %copy-done.46), kind=kOutput, calls=%fused_computation.82 | convolution fusion | flops 637014528 | bytes 76709888 | tf_op jit(solution)/shard_map/kgqj,kjd->kgqd/dot_general | solution.py:204
  977.2 45.3 %fusion.27 = f32[2,3,512,64]{2,3,1,0:T(8,128)} fusion(f32[2,3,512,2048]{3,2,1,0:T(8,128)} %fusion.214, f32[2,3,512,2048]{3,2,1,0:T(8,128)} %get-tuple-element.163, f32[2,3,512]{2,1,0:T(4,128)S(1)} %copy-done.78, pred[512,2048]{1,0:T(8,128)(4,1)} %copy-done.20, bf16[2048,2,32]{0,2,1:T(8,128)(2,1)S(1)} %copy-done.40, bf16[2048,2,32]{0,2,1:T(8,128)(2,1)S(1)} %copy-done.37), kind=kOutput, calls=%fused_computation.47 | convolution fusion | flops 875566080 | bytes 52703232 | tf_op jit(solution)/shard_map/kgqj,kjd->kgqd/dot_general | solution.py:204
  1041.2 12.5 add_convert_fusion
  1061.4 40.1 %all-reduce.6 = (f32[64]{0:T(128)}, f32[64]{0:T(128)}) all-reduce(f32[64]{0:T(128)S(1)} %get-tuple-element.129, f32[64]{0:T(128)S(1)} %get-tuple-element.131), channel_id=1, replica_groups=mesh['dp'=8,'tensor'=4] {'dp','tensor'}, use_global_device_ids=true, to_apply=%region_31.32 | all-reduce | flops 128 | bytes 1024 | tf_op jit(solution)/shard_map/psum | solution.py:239
  1101.6 12.7 all-reduce.19.cloned.1.call-done
  1138.5 406.0 %all-reduce.21.cloned.1.call-done = (bf16[2048,1536]{1,0:T(8,128)(2,1)}, bf16[2048,1536]{1,0:T(8,128)(2,1)}) async-done(((bf16[2048,1536]{1,0:T(8,128)(2,1)}, bf16[2048,1536]{1,0:T(8,128)(2,1)}), (bf16[2048,1536]{1,0:T(8,128)(2,1)}, bf16[2048,1536]{1,0:T(8,128)(2,1)})) %all-reduce.21.cloned.1.call-update) | async-done | bytes 12582928 | tf_op jit(solution)/shard_map/psum | solution.py:158
  1552.7 14.8 all-reduce.7
  1568.8 21.0 %fusion.34 = (f32[2048,1536]{1,0:T(8,128)}, bf16[2048,1536]{1,0:T(8,128)(2,1)}) fusion(f32[2048,1536]{1,0:T(8,128)} %copy-done.6, bf16[2048,1536]{1,0:T(8,128)(2,1)} %get-tuple-element.144, bf16[2048,1536]{1,0:T(8,128)(2,1)} %param.34, f32[2048]{0:T(1024)S(1)} %multiply_multiply_fusion.4, f32[1536]{0:T(1024)S(1)} %copy-done.57, f32[2048]{0:T(1024)S(1)} %copy-done.54, ...), kind=kLoop, calls=%fused_computation.53 | loop fusion | flops 40894464 | bytes 56645632 | tf_op jit(solution)/shard_map/add | solution.py:238
  1589.8 15.2 all-gather.3.cloned.1.call-done
  (320 shorter events, 307.7 us)
Async XLA Ops:
  7.2 101.9 %copy-start = (bf16[384,1536]{1,0:T(8,128)(2,1)S(1)}, bf16[384,1536]{1,0:T(8,128)(2,1)}, u32[]{:S(2)}) copy-start(bf16[384,1536]{1,0:T(8,128)(2,1)} %param.41) | copy-start | bytes 3538948
  7.2 333.1 %all-reduce.15.cloned.1.call-start = ((), (), s32[]{:S(2)}) async-start(), calls=%async_computation | async-start | bytes 12582912 | tf_op jit(solution)/shard_map/psum | solution.py:148
  19.2 76.8 %copy-start.12 = (bf16[2048,128]{0,1:T(8,128)(2,1)}, bf16[2048,128]{0,1:T(8,128)(2,1)S(1)}, u32[]{:S(2)}) copy-start(bf16[2048,128]{0,1:T(8,128)(2,1)S(1)} %convolution_convert_fusion.6) | copy-start | bytes 1572868
  27.8 45.7 %copy-start.36 = (bf16[2048,2,32]{0,2,1:T(8,128)(2,1)}, bf16[2048,2,32]{0,2,1:T(8,128)(2,1)S(1)}, u32[]{:S(2)}) copy-start(bf16[2048,2,32]{0,2,1:T(8,128)(2,1)S(1)} %get-tuple-element.156) | copy-start | bytes 786436
  28.9 44.6 %copy-start.28 = (bf16[2048,6,64]{0,2,1:T(8,128)(2,1)}, bf16[2048,6,64]{0,2,1:T(8,128)(2,1)S(1)}, u32[]{:S(2)}) copy-start(bf16[2048,6,64]{0,2,1:T(8,128)(2,1)S(1)} %pad_maximum_fusion.1) | copy-start | bytes 4718596
  114.5 233.2 %copy-start.62 = (f32[1536]{0:T(1024)S(1)}, f32[1536]{0:T(1024)}, u32[]{:S(2)}) copy-start(f32[1536]{0:T(1024)} %param.44) | copy-start | bytes 18436
  114.6 554.0 %all-reduce.17.cloned.1.call-start = ((), (), s32[]{:S(2)}) async-start(), calls=%async_computation.1 | async-start | bytes 12582912 | tf_op jit(solution)/shard_map/psum | solution.py:171
  446.6 667.7 %all-reduce.19.cloned.1.call-start = ((), (), s32[]{:S(2)}) async-start(), calls=%async_computation.3 | async-start | bytes 35782656 | tf_op jit(solution)/shard_map/psum | solution.py:243
  446.7 33.9 %slice-start.7 = ((s8[6291456]{0:T(1024)(128)(4,1)}), s8[4194304]{0:T(1024)(128)(4,1)S(1)}, s32[]{:S(2)}) async-start(s8[6291456]{0:T(1024)(128)(4,1)} %bitcast.204), calls=%async_computation.12 | async-start | bytes 8388608
  480.6 188.0 %copy-start.56 = (f32[2048]{0:T(1024)S(1)}, f32[2048]{0:T(1024)}, u32[]{:S(2)}) copy-start(f32[2048]{0:T(1024)} %copy-done.55) | copy-start | bytes 24580
  480.6 188.0 %copy-start.63 = (f32[1536]{0:T(1024)S(1)}, f32[1536]{0:T(1024)}, u32[]{:S(2)}) copy-start(f32[1536]{0:T(1024)} %param.44) | copy-start | bytes 18436
  493.9 184.9 %copy-start.61 = (f32[2048]{0:T(1024)S(1)}, f32[2048]{0:T(1024)}, u32[]{:S(2)}) copy-start(f32[2048]{0:T(1024)} %copy-done.60) | copy-start | bytes 24580
  825.5 48.9 %copy-start.15 = (f32[2048,32]{0,1:T(8,128)S(1)}, f32[2048,32]{0,1:T(8,128)}, u32[]{:S(2)}) copy-start(f32[2048,32]{0,1:T(8,128)} %copy-done.14) | copy-start | bytes 786436
  825.5 48.9 %copy-start.17 = (f32[2048,32]{0,1:T(8,128)S(1)}, f32[2048,32]{0,1:T(8,128)}, u32[]{:S(2)}) copy-start(f32[2048,32]{0,1:T(8,128)} %copy-done.16) | copy-start | bytes 786436
  825.5 50.2 %copy-start.8 = (f32[2048,128]{0,1:T(8,128)S(1)}, f32[2048,128]{0,1:T(8,128)}, u32[]{:S(2)}) copy-start(f32[2048,128]{0,1:T(8,128)} %copy-done.7) | copy-start | bytes 3145732
  825.5 50.2 %copy-start.50 = (f32[2048,2]{0,1:T(2,128)S(1)}, f32[2048,2]{0,1:T(2,128)}, u32[]{:S(2)}) copy-start(f32[2048,2]{0,1:T(2,128)} %copy-done.49) | copy-start | bytes 49156
  825.5 50.2 %copy-start.84 = (f32[64]{0:T(128)S(1)}, f32[64]{0:T(128)}, u32[]{:S(2)}) copy-start(f32[64]{0:T(128)} %param.43) | copy-start | bytes 772
  825.5 50.6 %copy-start.52 = (f32[2048,2]{0,1:T(2,128)S(1)}, f32[2048,2]{0,1:T(2,128)}, u32[]{:S(2)}) copy-start(f32[2048,2]{0,1:T(2,128)} %copy-done.51) | copy-start | bytes 49156
  881.9 662.6 %all-reduce.21.cloned.1.call-start = ((), (), s32[]{:S(2)}) async-start(), calls=%async_computation.4 | async-start | bytes 25165824 | tf_op jit(solution)/shard_map/psum | solution.py:158
  1053.8 551.2 %all-gather.3.cloned.1.call-start = ((), (), s32[]{:S(2)}) async-start(), calls=%async_computation.2 | async-start | bytes 10616832 | tf_op jit(solution)/shard_map/all_gather | solution.py:14
  1132.8 411.7 %copy-start.54 = (f32[2048]{0:T(1024)S(1)}, f32[2048]{0:T(1024)}, u32[]{:S(2)}) copy-start(f32[2048]{0:T(1024)} %copy-done.53) | copy-start | bytes 24580
  1132.8 411.7 %copy-start.57 = (f32[1536]{0:T(1024)S(1)}, f32[1536]{0:T(1024)}, u32[]{:S(2)}) copy-start(f32[1536]{0:T(1024)} %param.37) | copy-start | bytes 18436
  1138.5 414.2 %copy-start.80 = (bf16[1536]{0:T(1024)(128)(2,1)S(1)}, bf16[1536]{0:T(1024)(128)(2,1)}, u32[]{:S(2)}) copy-start(bf16[1536]{0:T(1024)(128)(2,1)} %get-tuple-element.125) | copy-start | bytes 9220
  1138.5 430.3 %copy-start.59 = (f32[2048]{0:T(1024)S(1)}, f32[2048]{0:T(1024)}, u32[]{:S(2)}) copy-start(f32[2048]{0:T(1024)} %copy-done.58) | copy-start | bytes 24580
  (85 other events, 755.4 us)
Sparse Core Ops, SparseCore 0:
  114.7 225.5 all-reduce.14
  446.7 221.7 all-reduce.16
  882.0 232.2 all-reduce.18
  1117.5 426.9 all-reduce.20
  1547.0 57.9 all-gather.2
